TPU v7x, 32 devices: a whole 2x2x4 slice. The times are simulated.
32 devices in a mesh: depth: 16 (over z, x, core), tile: 2 (over y).
Axes of the slice: x: 2, y: 2, z: 4, core: 2. Of those that a mesh axis runs over, the one named last changes fastest.
Arguments:
- density: bfloat16 [3, 128, 4, 4096], P(None, 'depth', 'tile'), may hold values from 0 to 1
- material_weight: float32 [4, 3], replicated, may hold values from 0.3 to 3
- color_table: int32 [4, 4, 256], replicated, may hold values from 0 to 255
Outputs:
- pixels: float32 [4, 4, 4, 4096], P(None, None, 'tile', 'depth')
Inputs may be any that keep to these rules, and one draw needn't show every extreme that they name: `color_table`: levels of a transfer function, 255 meaning full.
All inputs are finite; a program needn't handle non-finite values.
Results may differ from a plain program's by a relative error of at most 0.0003.
Values may be sent and summed in bfloat16 or wider, within the bound.
A program may use at most 128 MiB of HBM per device.

v0:
```python
import functools

import jax
import jax.numpy as jnp
from jax import lax
from jax.experimental import pallas as pl
from jax.experimental.pallas import tpu as pltpu
from jax.sharding import PartitionSpec as P

LANES = 128
SUB = 8


def pack_tables(table_ref, tabs):
    for e in range(table_ref.shape[0]):
        word = (
            table_ref[e, 0:1, :]
            + table_ref[e, 1:2, :] * 256
            + table_ref[e, 2:3, :] * 65536
            + lax.shift_left(table_ref[e, 3:4, :], 24)
        )
        bins = word.shape[1]
        pair = (word, pltpu.roll(word, bins - 1, 1))
        for k in range(2):
            for half in range(bins // LANES):
                tabs[e, k, half] = jnp.broadcast_to(
                    pair[k][:, half * LANES : (half + 1) * LANES], (SUB, LANES)
                )


def look_up(tabs, e, k, idx, where_half):
    found = None
    for half in range(tabs.shape[2]):
        piece = jnp.take_along_axis(tabs[e, k, half], idx, axis=1, mode="promise_in_bounds")
        found = piece if found is None else jnp.where(where_half == half, piece, found)
    return found


def channels_of(word):
    return (
        (word & 255).astype(jnp.float32),
        (lax.shift_right_logical(word, 8) & 255).astype(jnp.float32),
        (lax.shift_right_logical(word, 16) & 255).astype(jnp.float32),
        lax.shift_right_logical(word, 24).astype(jnp.float32),
    )


def mixer(weight_ref, e):
    w = [weight_ref[e, m] for m in range(weight_ref.shape[1])]

    def mix(values):
        total = w[0] * values[0]
        for m in range(1, len(values)):
            total = total + w[m] * values[m]
        return total

    return mix


def tile_levels(grid_ref, tabs, weight_ref, levels, y, tile, scale):
    mats, planes = grid_ref.shape[:2]
    for z in range(planes):
        mid = [grid_ref[m, z, y, tile].astype(jnp.float32) for m in range(mats)]
        for e in range(weight_ref.shape[0]):
            atten = mixer(weight_ref, e)(mid)
            level = 255.0 - 255.0 * jnp.exp(-0.5 * atten)
            bin_at = level.astype(jnp.int32)
            frac = level - bin_at.astype(jnp.float32)
            w1 = frac.astype(jnp.bfloat16).astype(jnp.float32)
            w0 = (1.0 - frac).astype(jnp.bfloat16).astype(jnp.float32)
            idx = bin_at & (LANES - 1)
            half = lax.shift_right_logical(bin_at, 7)
            low = channels_of(look_up(tabs, e, 0, idx, half))
            high = channels_of(look_up(tabs, e, 1, idx, half))
            for c in range(4):
                value = w0 * low[c] + w1 * high[c]
                levels[y, tile, z, e * 4 + c] = value * scale if c == 3 else value


def tile_image(dens, levels, weight_ref, y, tile, planes):
    mats = dens.shape[0]
    energies = weight_ref.shape[0]
    lane = lax.broadcasted_iota(jnp.int32, (SUB, LANES), 1)
    first, last = lane == 0, lane == LANES - 1
    base = tile * SUB + SUB
    rows = pl.ds(pl.multiple_of(base, SUB), SUB)
    ahead = [None] * energies
    sums = [[None] * 3 for _ in range(energies)]
    for z in range(planes):
        dz, dy, dx = [], [], []
        for m in range(mats):
            here = dens[m, z + 1, y + 1, rows, :]
            dz.append(dens[m, z + 2, y + 1, rows, :] - dens[m, z, y + 1, rows, :])
            dy.append(dens[m, z + 1, y + 2, rows, :] - dens[m, z + 1, y, rows, :])
            above = dens[m, z + 1, y + 1, pl.ds(base - 1, SUB), :]
            below = dens[m, z + 1, y + 1, pl.ds(base + 1, SUB), :]
            right = pltpu.roll(jnp.where(first, below, here), LANES - 1, 1)
            left = pltpu.roll(jnp.where(last, above, here), 1, 1)
            dx.append(right - left)
        for e in range(energies):
            mix = mixer(weight_ref, e)
            gz, gy, gx = mix(dz) * 0.5, mix(dy) * 0.5, mix(dx) * 0.5
            sq = gz * gz + gy * gy + gx * gx
            inv = lax.rsqrt(sq + 1.0)
            shading = 0.3 + 0.7 * jnp.abs(0.8 * gz + 0.48 * gy + 0.36 * gx) * inv
            opacity = levels[y, tile, z, e * 4 + 3] * (sq * inv * inv)
            lit = opacity * shading
            if z:
                lit = lit * ahead[e]
            for c in range(3):
                term = lit * levels[y, tile, z, e * 4 + c]
                sums[e][c] = term if z == 0 else sums[e][c] + term
            transmit = 1.0 - opacity
            ahead[e] = transmit if z == 0 else ahead[e] * transmit
    return sums, ahead


def far_first(mine, step, tiles):
    if tiles & (tiles - 1):
        return (mine + 1 + step) % tiles
    other, result, bit = tiles - 1 - step, 0, 1
    while bit < tiles:
        result = result + bit * ((mine // bit + other // bit) % 2)
        bit *= 2
    return result


def render_kernel(
    depth_total, mixed_ref, table_ref, weight_ref, out_ref,
    grid_ref, wide, dens, tabs, levels, z_in, y_in, image, pair_in, got,
    z_send, z_recv, y_send, y_recv, pair_send, pair_recv, send_sem, recv_sem,
):
    mats, planes, lines, tiles = grid_ref.shape[:4]
    strips = tiles * SUB
    energies = weight_ref.shape[0]
    pairs, block, _ = got.shape
    count = 2 * pairs
    per_tile = count // tiles
    half_tile = per_tile // 2
    group = energies * lines
    stride = 4 * group
    me, row = lax.axis_index("depth"), lax.axis_index("tile")
    rows_of = lax.axis_size("tile")
    has_z = (me > 0, me < count - 1)
    has_y = (row > 0, row < rows_of - 1)
    z_peer = (me - 1, me + 1)
    y_peer = (row - 1, row + 1)
    mine = me // per_tile
    core, pair = me % 2, me // 2
    partner = me + 1 - 2 * core

    barrier = pltpu.get_barrier_semaphore()

    def greet(o, carry):
        @pl.when(o != pair)
        def _():
            pl.semaphore_signal(
                barrier, inc=1, device_id={"depth": 2 * o + core},
                device_id_type=pl.DeviceIdType.MESH,
            )
        return carry

    for side in range(2):
        @pl.when(has_y[side])
        def _():
            pl.semaphore_signal(
                barrier, inc=1, device_id={"tile": y_peer[side]},
                device_id_type=pl.DeviceIdType.MESH,
            )

        @pl.when(has_z[side])
        def _():
            pl.semaphore_signal(
                barrier, inc=1, device_id={"depth": z_peer[side]},
                device_id_type=pl.DeviceIdType.MESH,
            )
    lax.fori_loop(0, pairs, greet, 0)

    pack_tables(table_ref, tabs)
    edge = jnp.zeros((SUB, LANES), jnp.float32)
    blank = jnp.zeros((strips + 2 * SUB, LANES), jnp.float32)

    def widen(z, carry):
        for m in range(mats):
            wide[m] = mixed_ref[m, z].astype(jnp.float32)
            for y in range(lines):
                dens[m, z + 1, y + 1, 0:SUB, :] = edge
                dens[m, z + 1, y + 1, SUB + strips :, :] = edge
                for t in range(tiles):
                    line = wide[m, pl.ds(t * SUB * lines + y, SUB, stride=lines), :]
                    dens[m, z + 1, y + 1, SUB + t * SUB : 2 * SUB + t * SUB, :] = line
                    grid_ref[m, z, y, t] = line.astype(grid_ref.dtype)
        for side in range(2):
            @pl.when(jnp.logical_not(has_y[side]))
            def _():
                for m in range(mats):
                    dens[m, z + 1, side * (lines + 1)] = blank
        return carry

    lax.fori_loop(0, planes, widen, 0)
    for side in range(2):
        @pl.when(jnp.logical_not(has_z[side]))
        def _():
            for m in range(mats):
                for y in range(lines):
                    dens[m, side * (planes + 1), y + 1] = blank

    def level_step(j, carry):
        tile_levels(
            grid_ref, tabs, weight_ref, levels, j % lines, j // lines, 6.0 / depth_total / 255.0
        )
        return carry

    early = tiles * lines // 2
    lax.fori_loop(0, early, level_step, 0)

    others = pairs - 1
    for side in range(2):
        others = others + jnp.where(has_y[side], 1, 0) + jnp.where(has_z[side], 1, 0)
    pl.semaphore_wait(barrier, others)

    def z_copy(side):
        return pltpu.make_async_remote_copy(
            src_ref=grid_ref.at[:, (planes - 1) * side],
            dst_ref=z_in.at[1 - side],
            send_sem=z_send.at[side],
            recv_sem=z_recv.at[1 - side],
            device_id={"depth": z_peer[side]},
            device_id_type=pl.DeviceIdType.MESH,
        )

    def y_copy(side, t):
        return pltpu.make_async_remote_copy(
            src_ref=grid_ref.at[:, :, (lines - 1) * side, t],
            dst_ref=y_in.at[1 - side, t],
            send_sem=y_send.at[side, t],
            recv_sem=y_recv.at[1 - side, t],
            device_id={"tile": y_peer[side]},
            device_id_type=pl.DeviceIdType.MESH,
        )

    def rows_of_block(owner):
        return pl.ds(pl.multiple_of(owner * block, block), block)

    def pair_copy(chip):
        return pltpu.make_async_remote_copy(
            src_ref=image.at[rows_of_block(2 * chip + 1 - core)],
            dst_ref=pair_in.at[chip],
            send_sem=pair_send.at[chip],
            recv_sem=pair_recv.at[chip],
            device_id={"depth": partner},
            device_id_type=pl.DeviceIdType.MESH,
        )

    def block_copy(chip, source):
        return pltpu.make_async_remote_copy(
            src_ref=image.at[rows_of_block(2 * chip + core)],
            dst_ref=got.at[source],
            send_sem=send_sem.at[chip],
            recv_sem=recv_sem.at[source],
            device_id={"depth": 2 * chip + core},
            device_id_type=pl.DeviceIdType.MESH,
        )

    def forward(i):
        tile = far_first(mine, i, tiles)
        for k in range(half_tile):
            chip = tile * half_tile + k
            pair_copy(chip).wait_recv()
            start = (2 * chip + core) * block
            for s in range(block // stride):
                at = [
                    pl.ds(pl.multiple_of(start + (s * 4 + c) * group, group), group)
                    for c in range(4)
                ]
                ours = [image[at[c], :] for c in range(4)]
                theirs = [
                    pair_in[chip, (s * 4 + c) * group : (s * 4 + c + 1) * group, :]
                    for c in range(4)
                ]
                front = [jnp.where(core == 0, a, b) for a, b in zip(ours, theirs)]
                back = [jnp.where(core == 0, b, a) for a, b in zip(ours, theirs)]
                for c in range(3):
                    image[at[c], :] = front[c] + front[3] * back[c]
                image[at[3], :] = front[3] * back[3]

            @pl.when(chip != pair)
            def _():
                block_copy(chip, pair).start()

    for side in range(2):
        @pl.when(has_z[side])
        def _():
            z_copy(side).start()
    for i in range(tiles):
        for side in range(2):
            @pl.when(has_y[side])
            def _():
                y_copy(side, far_first(mine, i, tiles)).start()

    lax.fori_loop(early, tiles * lines, level_step, 0)

    for side in range(2):
        @pl.when(has_z[side])
        def _():
            z_copy(1 - side).wait_recv()
            for t in range(tiles):
                for m in range(mats):
                    for y in range(lines):
                        dens[
                            m, side * (planes + 1), y + 1, SUB + t * SUB : 2 * SUB + t * SUB, :
                        ] = z_in[side, m, y, t].astype(jnp.float32)

    def tile_step(i, carry):
        tile = far_first(mine, i, tiles)
        here = pl.ds(pl.multiple_of(tile * SUB + SUB, SUB), SUB)
        for side in range(2):
            @pl.when(has_y[side])
            def _():
                y_copy(1 - side, tile).wait_recv()
                for m in range(mats):
                    for z in range(planes):
                        dens[m, z + 1, side * (lines + 1), here, :] = y_in[
                            side, tile, m, z
                        ].astype(jnp.float32)

        def line_step(y, inner):
            sums, ahead = tile_image(
                dens, levels, weight_ref, y, tile, planes
            )
            for e in range(energies):
                for c in range(4):
                    value = sums[e][c] * (1.0 / 255.0) if c < 3 else ahead[e]
                    start = tile * (SUB * stride) + c * group + e * lines + y
                    image[pl.ds(start, SUB, stride=stride), :] = value
            return inner

        lax.fori_loop(0, lines, line_step, 0)
        for k in range(half_tile):
            pair_copy(tile * half_tile + k).start()

        @pl.when(i > 0)
        def _():
            forward(i - 1)
        return carry

    lax.fori_loop(0, tiles, tile_step, 0)
    forward(tiles - 1)
    got[pair] = image[rows_of_block(me), :]

    pieces = block // stride
    ahead = [None] * pieces
    sums = [[None] * 3 for _ in range(pieces)]
    for n in range(pairs):
        @pl.when(pair != n)
        def _():
            block_copy(n, n).wait_recv()
        for s in range(pieces):
            at = lambda c: got[n, (s * 4 + c) * group : (s * 4 + c + 1) * group, :]
            for c in range(3):
                sums[s][c] = at(c) if n == 0 else sums[s][c] + ahead[s] * at(c)
            ahead[s] = at(3) if n == 0 else ahead[s] * at(3)
    for s in range(pieces):
        for c in range(4):
            value = sums[s][c] if c < 3 else 1.0 - ahead[s]
            for e in range(energies):
                start = ((e * 4 + c) * pieces + s) * lines
                out_ref[start : start + lines, :] = value[e * lines : (e + 1) * lines, :]

    for side in range(2):
        @pl.when(has_z[side])
        def _():
            z_copy(side).wait_send()
        @pl.when(has_y[side])
        def _():
            for t in range(tiles):
                y_copy(side, t).wait_send()
    for n in range(pairs):
        pair_copy(n).wait_send()

        @pl.when(pair != n)
        def _():
            block_copy(n, n).wait_send()


def body(density, material_weight, color_table):
    mats, planes, lines, columns = density.shape
    energies = material_weight.shape[0]
    count = lax.axis_size("depth")
    strips = columns // LANES
    tiles = strips // SUB
    mixed = density.reshape(mats, planes, lines, strips, LANES).transpose(0, 1, 3, 2, 4)
    mixed = mixed.reshape(mats, planes, strips * lines, LANES)
    vmem = pl.BlockSpec(memory_space=pltpu.VMEM)
    total = strips * 4 * energies * lines
    own = columns // count
    dma = pltpu.SemaphoreType.DMA
    pixels = pl.pallas_call(
        functools.partial(render_kernel, planes * count),
        out_shape=jax.ShapeDtypeStruct((total // count, LANES), jnp.float32),
        in_specs=[vmem, vmem, pl.BlockSpec(memory_space=pltpu.SMEM)],
        out_specs=vmem,
        scratch_shapes=[
            pltpu.VMEM((mats, planes, lines, tiles, SUB, LANES), density.dtype),
            pltpu.VMEM((mats, strips * lines, LANES), jnp.float32),
            pltpu.VMEM((mats, planes + 2, lines + 2, strips + 2 * SUB, LANES), jnp.float32),
            pltpu.VMEM((energies, 2, color_table.shape[2] // LANES, SUB, LANES), jnp.int32),
            pltpu.VMEM((lines, tiles, planes, energies * 4, SUB, LANES), jnp.float32),
            pltpu.VMEM((2, mats, lines, tiles, SUB, LANES), density.dtype),
            pltpu.VMEM((2, tiles, mats, planes, SUB, LANES), density.dtype),
            pltpu.VMEM((total, LANES), jnp.float32),
            pltpu.VMEM((count // 2, total // count, LANES), jnp.float32),
            pltpu.VMEM((count // 2, total // count, LANES), jnp.float32),
            dma((2,)), dma((2,)), dma((2, tiles)), dma((2, tiles)),
            dma((count // 2,)), dma((count // 2,)), dma((count // 2,)), dma((count // 2,)),
        ],
        compiler_params=pltpu.CompilerParams(collective_id=0, has_side_effects=True),
    )(mixed, color_table, material_weight)
    pixels = pixels.reshape(energies, 4, own // LANES, lines, LANES)
    return pixels.transpose(0, 1, 3, 2, 4).reshape(energies, 4, lines, own)


def solution(mesh):
    return jax.shard_map(
        body,
        mesh=mesh,
        in_specs=(P(None, "depth", "tile", None), P(), P()),
        out_specs=P(None, None, "tile", "depth"),
        check_vma=False,
    )
```

profile of v0, /device:TPU:0, one launch (start us, length us, event | category | flops | bytes accessed | tf_op | source)
XLA Modules:
  0.0 22.4 jit_solution(13101160017269341672)
XLA Ops:
  0.0 21.0 %shard_map.37 = f32[64,128]{1,0:T(8,128)} custom-call(bf16[3,8,64,128]{3,2,1,0:T(8,128)(2,1)} %bitcast.10, s32[4,4,256]{2,1,0:T(4,128)} %table_ref.1, f32[4,3]{1,0:T(4,128)} %weight_ref.1), custom_call_target="tpu_custom_call" | custom-call | tf_op jit(solution)/shard_map/pallas_call | solution.py:398
  21.0 1.4 %copy.7 = f32[4,4,2,256]{3,2,1,0:T(2,128)} copy(f32[4,4,2,256]{3,2,1,0:T(2,128)} %bitcast.11) | data formatting | bytes 65536
where the time goes:
time: 22.6 us; the launch traced here: 22.4 us
  Pallas kernels  21 us (93%)
  local copies, waits for them, and re-layouts  1.38 us (6%)
    pallas_call x1, Pallas kernels, body(): pl.pallas_call(functools.partial(render_kernel, planes * count), out_shap...  21 us
    unnamed x1, local copies, waits for them, and re-layouts  1.38 us

commit v1 on v0

--- a/solution.py
+++ b/solution.py
@@ -397,7 +397,7 @@
     dma = pltpu.SemaphoreType.DMA
     pixels = pl.pallas_call(
         functools.partial(render_kernel, planes * count),
-        out_shape=jax.ShapeDtypeStruct((total // count, LANES), jnp.float32),
+        out_shape=pltpu.VMEM((total // count, LANES), jnp.float32),
         in_specs=[vmem, vmem, pl.BlockSpec(memory_space=pltpu.SMEM)],
         out_specs=vmem,
         scratch_shapes=[

time: 22.6 us -> 21.2 us (0.938)
  local copies, waits for them, and re-layouts: 1.38 us -> 0.62 us
  Pallas kernels: 21 us -> 20.4 us
    unnamed x1, local copies, waits for them, and re-layouts: 1.38 us -> 0.62 us
    pallas_call x1, Pallas kernels: 21 us -> 20.4 us  [body(): pl.pallas_call(functools.partial(render_kernel, planes * count), out_shap...]
where the time goes in v1:
time: 21.2 us; the launch traced here: 21 us
  Pallas kernels  20.4 us (96%)
  local copies, waits for them, and re-layouts  0.62 us (3%)
    pallas_call x1, Pallas kernels, body(): pl.pallas_call(functools.partial(render_kernel, planes * count), out_shap...  20.4 us
    unnamed x1, local copies, waits for them, and re-layouts  0.62 us

profile of v1, /device:TPU:0, one launch (start us, length us, event | category | flops | bytes accessed | tf_op | source)
XLA Modules:
  0.0 21.0 jit_solution(5850872597318676843)
XLA Ops:
  0.0 20.4 %shard_map.37 = f32[64,128]{1,0:T(8,128)S(1)} custom-call(bf16[3,8,64,128]{3,2,1,0:T(8,128)(2,1)} %bitcast.11, s32[4,4,256]{2,1,0:T(4,128)} %table_ref.1, f32[4,3]{1,0:T(4,128)} %weight_ref.1), custom_call_target="tpu_custom_call" | custom-call | tf_op jit(solution)/shard_map/pallas_call | solution.py:398
  20.4 0.6 %copy.7 = f32[4,4,2,256]{3,2,1,0:T(2,128)} copy(f32[4,4,2,256]{3,2,1,0:T(2,128)S(1)} %bitcast.10) | data formatting | bytes 65536

commit v2 on v1

--- a/solution.py
+++ b/solution.py
@@ -125,20 +125,38 @@
     return result
 
 
+WIRE_STEPS = 64000.0
+WIRE_ZERO = 32768
+
+
+def to_wire(value):
+    root = jnp.sqrt(jnp.sqrt(jnp.maximum(value, 0.0)))
+    return (root * WIRE_STEPS + 0.5).astype(jnp.int32) - WIRE_ZERO
+
+
+def from_wire(code):
+    root = (code.astype(jnp.float32) + float(WIRE_ZERO)) * (1.0 / WIRE_STEPS)
+    root = root * root
+    return root * root
+
+
 def render_kernel(
-    depth_total, mixed_ref, table_ref, weight_ref, out_ref,
-    grid_ref, wide, dens, tabs, levels, z_in, y_in, image, pair_in, got,
+    depth_total, mixed_hbm, table_hbm, weight_hbm, out_ref,
+    mixed_ref, table_ref, weight_ref,
+    grid_ref, wide, dens, tabs, levels, z_in, y_in, image, pair_in, packed, got,
+    in_sem, up_sem, down_sem, side_sem,
     z_send, z_recv, y_send, y_recv, pair_send, pair_recv, send_sem, recv_sem,
 ):
     mats, planes, lines, tiles = grid_ref.shape[:4]
     strips = tiles * SUB
     energies = weight_ref.shape[0]
-    pairs, block, _ = got.shape
+    _, pairs, block, _ = got.shape
     count = 2 * pairs
     per_tile = count // tiles
     half_tile = per_tile // 2
-    group = energies * lines
-    stride = 4 * group
+    stride = 4 * energies
+    pieces = block // stride
+    line_rows = strips * stride
     me, row = lax.axis_index("depth"), lax.axis_index("tile")
     rows_of = lax.axis_size("tile")
     has_z = (me > 0, me < count - 1)
@@ -148,37 +166,60 @@
     mine = me // per_tile
     core, pair = me % 2, me // 2
     partner = me + 1 - 2 * core
+    beside = me + 2 - 4 * (pair % 2)
+    layers = pairs // 2
+    layer = pair // 2
+    has_layer = (layer > 0, layer < layers - 1)
+    layer_peer = (me - 4, me + 4)
+    first_line = jnp.where(has_y[0], 1, 0)
+
+    def line_of(k):
+        return (k + first_line) % lines
+
+    loads = (
+        pltpu.make_async_copy(mixed_hbm, mixed_ref, in_sem.at[0]),
+        pltpu.make_async_copy(table_hbm, table_ref, in_sem.at[1]),
+        pltpu.make_async_copy(weight_hbm, weight_ref, in_sem.at[2]),
+    )
+    for load in loads:
+        load.start()
 
     barrier = pltpu.get_barrier_semaphore()
 
-    def greet(o, carry):
-        @pl.when(o != pair)
-        def _():
-            pl.semaphore_signal(
-                barrier, inc=1, device_id={"depth": 2 * o + core},
-                device_id_type=pl.DeviceIdType.MESH,
-            )
-        return carry
-
+    def tell(semaphore, **device):
+        pl.semaphore_signal(
+            semaphore, inc=1, device_id=device, device_id_type=pl.DeviceIdType.MESH
+        )
+
+    tell(barrier, depth=partner)
+    tell(barrier, depth=beside)
+    others = 2
+    outer = me - 1 + 2 * core
+    has_outer = jnp.logical_and(outer >= 0, outer < count)
+
+    @pl.when(has_outer)
+    def _():
+        tell(barrier, depth=outer)
+    others = others + jnp.where(has_outer, 1, 0)
     for side in range(2):
         @pl.when(has_y[side])
         def _():
-            pl.semaphore_signal(
-                barrier, inc=1, device_id={"tile": y_peer[side]},
-                device_id_type=pl.DeviceIdType.MESH,
-            )
-
-        @pl.when(has_z[side])
-        def _():
-            pl.semaphore_signal(
-                barrier, inc=1, device_id={"depth": z_peer[side]},
-                device_id_type=pl.DeviceIdType.MESH,
-            )
-    lax.fori_loop(0, pairs, greet, 0)
-
-    pack_tables(table_ref, tabs)
+            tell(barrier, tile=y_peer[side])
+
+        @pl.when(has_layer[side])
+        def _():
+            tell(barrier, depth=layer_peer[side])
+        others = others + jnp.where(has_y[side], 1, 0) + jnp.where(has_layer[side], 1, 0)
+
     edge = jnp.zeros((SUB, LANES), jnp.float32)
     blank = jnp.zeros((strips + 2 * SUB, LANES), jnp.float32)
+    for side in range(2):
+        @pl.when(jnp.logical_not(has_z[side]))
+        def _():
+            for m in range(mats):
+                for y in range(lines):
+                    dens[m, side * (planes + 1), y + 1] = blank
+    loads[0].wait()
 
     def widen(z, carry):
         for m in range(mats):
@@ -198,25 +239,6 @@
         return carry
 
     lax.fori_loop(0, planes, widen, 0)
-    for side in range(2):
-        @pl.when(jnp.logical_not(has_z[side]))
-        def _():
-            for m in range(mats):
-                for y in range(lines):
-                    dens[m, side * (planes + 1), y + 1] = blank
-
-    def level_step(j, carry):
-        tile_levels(
-            grid_ref, tabs, weight_ref, levels, j % lines, j // lines, 6.0 / depth_total / 255.0
-        )
-        return carry
-
-    early = tiles * lines // 2
-    lax.fori_loop(0, early, level_step, 0)
-
-    others = pairs - 1
-    for side in range(2):
-        others = others + jnp.where(has_y[side], 1, 0) + jnp.where(has_z[side], 1, 0)
     pl.semaphore_wait(barrier, others)
 
     def z_copy(side):
@@ -239,66 +261,104 @@
             device_id_type=pl.DeviceIdType.MESH,
         )
 
-    def rows_of_block(owner):
-        return pl.ds(pl.multiple_of(owner * block, block), block)
-
-    def pair_copy(chip):
+    def rows_of_block(y, owner):
+        return pl.ds(pl.multiple_of(y * line_rows + owner * block, block), block)
+
+    def pair_copy(y, chip):
         return pltpu.make_async_remote_copy(
-            src_ref=image.at[rows_of_block(2 * chip + 1 - core)],
-            dst_ref=pair_in.at[chip],
-            send_sem=pair_send.at[chip],
-            recv_sem=pair_recv.at[chip],
+            src_ref=image.at[rows_of_block(y, 2 * chip + 1 - core)],
+            dst_ref=pair_in.at[y, chip],
+            send_sem=pair_send.at[y, chip],
+            recv_sem=pair_recv.at[y, chip],
             device_id={"depth": partner},
             device_id_type=pl.DeviceIdType.MESH,
         )
 
-    def block_copy(chip, source):
+    def block_copy(y, chip, source):
         return pltpu.make_async_remote_copy(
-            src_ref=image.at[rows_of_block(2 * chip + core)],
-            dst_ref=got.at[source],
-            send_sem=send_sem.at[chip],
-            recv_sem=recv_sem.at[source],
+            src_ref=packed.at[y, chip],
+            dst_ref=got.at[y, source],
+            send_sem=send_sem.at[y, chip],
+            recv_sem=recv_sem.at[y, source],
             device_id={"depth": 2 * chip + core},
             device_id_type=pl.DeviceIdType.MESH,
         )
 
-    def forward(i):
-        tile = far_first(mine, i, tiles)
-        for k in range(half_tile):
-            chip = tile * half_tile + k
-            pair_copy(chip).wait_recv()
-            start = (2 * chip + core) * block
-            for s in range(block // stride):
-                at = [
-                    pl.ds(pl.multiple_of(start + (s * 4 + c) * group, group), group)
-                    for c in range(4)
-                ]
-                ours = [image[at[c], :] for c in range(4)]
-                theirs = [
-                    pair_in[chip, (s * 4 + c) * group : (s * 4 + c + 1) * group, :]
-                    for c in range(4)
-                ]
-                front = [jnp.where(core == 0, a, b) for a, b in zip(ours, theirs)]
-                back = [jnp.where(core == 0, b, a) for a, b in zip(ours, theirs)]
-                for c in range(3):
-                    image[at[c], :] = front[c] + front[3] * back[c]
-                image[at[3], :] = front[3] * back[3]
+    upper = lax.broadcasted_iota(jnp.int32, (SUB, LANES), 0) < energies
+
+    def both_halves(value):
+        return jnp.where(upper, pltpu.roll(value, energies, 0), value)
+
+    def forward(k):
+        y, tile = line_of(k // tiles), far_first(mine, k % tiles, tiles)
+        for h in range(half_tile):
+            chip = tile * half_tile + h
+            pair_copy(y, chip).wait_recv()
+            start = y * line_rows + (2 * chip + core) * block
+            for s in range(pieces):
+                front, back = [], []
+                for v in range(2):
+                    at = s * stride + v * SUB
+                    ours = image[pl.ds(pl.multiple_of(start + at, SUB), SUB), :]
+                    theirs = pair_in[y, chip, at : at + SUB, :]
+                    front.append(jnp.where(core == 0, ours, theirs))
+                    back.append(jnp.where(core == 0, theirs, ours))
+                clear = both_halves(front[1])
+                low = front[0] + clear * back[0]
+                high = jnp.where(upper, front[1], 0.0) + clear * back[1]
+                high = jnp.where(upper, high, 1.0 - high)
+                packed[y, chip, s * stride : (s + 1) * stride, :] = to_wire(
+                    jnp.concatenate([low, high], axis=0)
+                ).astype(packed.dtype)
 
             @pl.when(chip != pair)
             def _():
-                block_copy(chip, pair).start()
-
-    for side in range(2):
-        @pl.when(has_z[side])
-        def _():
-            z_copy(side).start()
+                block_copy(y, chip, pair).start()
+
     for i in range(tiles):
         for side in range(2):
             @pl.when(has_y[side])
             def _():
                 y_copy(side, far_first(mine, i, tiles)).start()
-
-    lax.fori_loop(early, tiles * lines, level_step, 0)
+        if i == 0:
+            for side in range(2):
+                @pl.when(has_z[side])
+                def _():
+                    z_copy(side).start()
+
+    loads[1].wait()
+    loads[2].wait()
+    pack_tables(table_ref, tabs)
+    steps = tiles * lines
+    every = max(1, steps // layers)
+
+    def pass_on(p):
+        for side, (turn, semaphore) in enumerate(((layers - 1 - layer, down_sem), (layer, up_sem))):
+            @pl.when(jnp.logical_and(turn == p, has_layer[1 - side]))
+            def _():
+                pl.semaphore_wait(semaphore, 1)
+
+            @pl.when(jnp.logical_and(turn == p, has_layer[side]))
+            def _():
+                tell(semaphore, depth=layer_peer[side])
+
+    def level_step(j, carry):
+        for p in range(layers):
+            if p * every < steps:
+                @pl.when(j == p * every)
+                def _():
+                    pass_on(p)
+        tile_levels(
+            grid_ref, tabs, weight_ref, levels, line_of(j // tiles), j % tiles,
+            6.0 / depth_total / 255.0,
+        )
+        return carry
+
+    lax.fori_loop(0, steps, level_step, 0)
+    for p in range(layers):
+        if p * every >= steps:
+            pass_on(p)
+    tell(side_sem, depth=beside)
 
     for side in range(2):
         @pl.when(has_z[side])
@@ -311,11 +371,11 @@
                             m, side * (planes + 1), y + 1, SUB + t * SUB : 2 * SUB + t * SUB, :
                         ] = z_in[side, m, y, t].astype(jnp.float32)
 
-    def tile_step(i, carry):
-        tile = far_first(mine, i, tiles)
+    def image_step(k, carry):
+        y, tile = line_of(k // tiles), far_first(mine, k % tiles, tiles)
         here = pl.ds(pl.multiple_of(tile * SUB + SUB, SUB), SUB)
         for side in range(2):
-            @pl.when(has_y[side])
+            @pl.when(jnp.logical_and(has_y[side], y == side * (lines - 1)))
             def _():
                 y_copy(1 - side, tile).wait_recv()
                 for m in range(mats):
@@ -324,48 +384,52 @@
                             side, tile, m, z
                         ].astype(jnp.float32)
 
-        def line_step(y, inner):
-            sums, ahead = tile_image(
-                dens, levels, weight_ref, y, tile, planes
-            )
-            for e in range(energies):
-                for c in range(4):
-                    value = sums[e][c] * (1.0 / 255.0) if c < 3 else ahead[e]
-                    start = tile * (SUB * stride) + c * group + e * lines + y
-                    image[pl.ds(start, SUB, stride=stride), :] = value
-            return inner
-
-        lax.fori_loop(0, lines, line_step, 0)
-        for k in range(half_tile):
-            pair_copy(tile * half_tile + k).start()
-
-        @pl.when(i > 0)
-        def _():
-            forward(i - 1)
+        sums, ahead = tile_image(dens, levels, weight_ref, y, tile, planes)
+        for e in range(energies):
+            for c in range(4):
+                value = sums[e][c] * (1.0 / 255.0) if c < 3 else ahead[e]
+                start = y * line_rows + tile * (SUB * stride) + c * energies + e
+                image[pl.ds(start, SUB, stride=stride), :] = value
+        for h in range(half_tile):
+            pair_copy(y, tile * half_tile + h).start()
+
+        @pl.when(k == 1)
+        def _():
+            pl.semaphore_wait(side_sem, 1)
+
+        @pl.when(k > 0)
+        def _():
+            forward(k - 1)
         return carry
 
-    lax.fori_loop(0, tiles, tile_step, 0)
-    forward(tiles - 1)
-    got[pair] = image[rows_of_block(me), :]
-
-    pieces = block // stride
-    ahead = [None] * pieces
-    sums = [[None] * 3 for _ in range(pieces)]
-    for n in range(pairs):
-        @pl.when(pair != n)
-        def _():
-            block_copy(n, n).wait_recv()
+    lax.fori_loop(0, steps, image_step, 0)
+    forward(steps - 1)
+    for y in range(lines):
+        got[y, pair] = packed[y, pair]
+
+    for k in range(lines):
+        y = line_of(k)
+        low, high, clear = [None] * pieces, [None] * pieces, [None] * pieces
+        for n in range(pairs):
+            @pl.when(pair != n)
+            def _():
+                block_copy(y, n, n).wait_recv()
+            for s in range(pieces):
+                both = from_wire(
+                    got[y, n, s * stride : (s + 1) * stride, :].astype(jnp.int32)
+                )
+                a, b = both[0:SUB], both[SUB:]
+                seen = both_halves(1.0 - b)
+                low[s] = a if n == 0 else low[s] + clear[s] * a
+                high[s] = b if n == 0 else high[s] + clear[s] * b
+                clear[s] = seen if n == 0 else clear[s] * seen
         for s in range(pieces):
-            at = lambda c: got[n, (s * 4 + c) * group : (s * 4 + c + 1) * group, :]
-            for c in range(3):
-                sums[s][c] = at(c) if n == 0 else sums[s][c] + ahead[s] * at(c)
-            ahead[s] = at(3) if n == 0 else ahead[s] * at(3)
-    for s in range(pieces):
-        for c in range(4):
-            value = sums[s][c] if c < 3 else 1.0 - ahead[s]
-            for e in range(energies):
-                start = ((e * 4 + c) * pieces + s) * lines
-                out_ref[start : start + lines, :] = value[e * lines : (e + 1) * lines, :]
+            parts = (low[s], jnp.where(upper, high[s], 1.0 - clear[s]))
+            for c in range(4):
+                value = parts[c // 2][(c % 2) * energies : (c % 2 + 1) * energies]
+                out_ref[
+                    pl.ds((c * pieces + s) * lines + y, energies, stride=4 * pieces * lines), :
+                ] = value
 
     for side in range(2):
         @pl.when(has_z[side])
@@ -375,12 +439,13 @@
         def _():
             for t in range(tiles):
                 y_copy(side, t).wait_send()
-    for n in range(pairs):
-        pair_copy(n).wait_send()
-
-        @pl.when(pair != n)
-        def _():
-            block_copy(n, n).wait_send()
+    for y in range(lines):
+        for n in range(pairs):
+            pair_copy(y, n).wait_send()
+
+            @pl.when(pair != n)
+            def _():
+                block_copy(y, n, n).wait_send()
 
 
 def body(density, material_weight, color_table):
@@ -391,16 +456,23 @@
     tiles = strips // SUB
     mixed = density.reshape(mats, planes, lines, strips, LANES).transpose(0, 1, 3, 2, 4)
     mixed = mixed.reshape(mats, planes, strips * lines, LANES)
-    vmem = pl.BlockSpec(memory_space=pltpu.VMEM)
+    hbm = pl.BlockSpec(memory_space=pl.ANY)
     total = strips * 4 * energies * lines
     own = columns // count
+    block = total // count // lines
+    pairs = count // 2
     dma = pltpu.SemaphoreType.DMA
+    flag = pltpu.SemaphoreType.REGULAR
+    wire = jnp.int16
     pixels = pl.pallas_call(
         functools.partial(render_kernel, planes * count),
         out_shape=pltpu.VMEM((total // count, LANES), jnp.float32),
-        in_specs=[vmem, vmem, pl.BlockSpec(memory_space=pltpu.SMEM)],
-        out_specs=vmem,
+        in_specs=[hbm, hbm, hbm],
+        out_specs=pl.BlockSpec(memory_space=pltpu.VMEM),
         scratch_shapes=[
+            pltpu.VMEM(mixed.shape, density.dtype),
+            pltpu.VMEM(color_table.shape, color_table.dtype),
+            pltpu.SMEM(material_weight.shape, material_weight.dtype),
             pltpu.VMEM((mats, planes, lines, tiles, SUB, LANES), density.dtype),
             pltpu.VMEM((mats, strips * lines, LANES), jnp.float32),
             pltpu.VMEM((mats, planes + 2, lines + 2, strips + 2 * SUB, LANES), jnp.float32),
@@ -409,10 +481,12 @@
             pltpu.VMEM((2, mats, lines, tiles, SUB, LANES), density.dtype),
             pltpu.VMEM((2, tiles, mats, planes, SUB, LANES), density.dtype),
             pltpu.VMEM((total, LANES), jnp.float32),
-            pltpu.VMEM((count // 2, total // count, LANES), jnp.float32),
-            pltpu.VMEM((count // 2, total // count, LANES), jnp.float32),
+            pltpu.VMEM((lines, pairs, block, LANES), jnp.float32),
+            pltpu.VMEM((lines, pairs, block, LANES), wire),
+            pltpu.VMEM((lines, pairs, block, LANES), wire),
+            dma((3,)), flag, flag, flag,
             dma((2,)), dma((2,)), dma((2, tiles)), dma((2, tiles)),
-            dma((count // 2,)), dma((count // 2,)), dma((count // 2,)), dma((count // 2,)),
+            dma((lines, pairs)), dma((lines, pairs)), dma((lines, pairs)), dma((lines, pairs)),
         ],
         compiler_params=pltpu.CompilerParams(collective_id=0, has_side_effects=True),
     )(mixed, color_table, material_weight)

time: 21.2 us -> 18.9 us (0.89)
  Pallas kernels: 20.4 us -> 18.1 us
    pallas_call x1, Pallas kernels: 20.4 us -> 18.1 us  [body(): pl.pallas_call(functools.partial(render_kernel, planes * count), out_shap...]
where the time goes in v2:
time: 18.9 us; the launch traced here: 18.7 us
  Pallas kernels  18.1 us (96%)
  local copies, waits for them, and re-layouts  0.62 us (3%)
    pallas_call x1, Pallas kernels, body(): pl.pallas_call(functools.partial(render_kernel, planes * count), out_shap...  18.1 us
    unnamed x1, local copies, waits for them, and re-layouts  0.62 us

profile of v2, /device:TPU:0, one launch (start us, length us, event | category | flops | bytes accessed | tf_op | source)
XLA Modules:
  0.0 18.7 jit_solution(18034782843582114432)
XLA Ops:
  0.0 18.1 %shard_map.37 = f32[64,128]{1,0:T(8,128)S(1)} custom-call(bf16[3,8,64,128]{3,2,1,0:T(8,128)(2,1)} %bitcast.11, s32[4,4,256]{2,1,0:T(4,128)} %table_hbm.1, f32[4,3]{1,0:T(4,128)} %weight_hbm.1), custom_call_target="tpu_custom_call" | custom-call | tf_op jit(solution)/shard_map/pallas_call | solution.py:467
  18.1 0.6 %copy.7 = f32[4,4,2,256]{3,2,1,0:T(2,128)} copy(f32[4,4,2,256]{3,2,1,0:T(2,128)S(1)} %bitcast.10) | data formatting | bytes 65536

commit v3 on v2

--- a/solution.py
+++ b/solution.py
@@ -9,6 +9,15 @@
 
 LANES = 128
 SUB = 8
+LAG = 4
+LOG2_E = 1.4426950408889634
+PICK = lax.GatherDimensionNumbers(
+    offset_dims=(),
+    collapsed_slice_dims=(1,),
+    start_index_map=(1,),
+    operand_batching_dims=(0,),
+    start_indices_batching_dims=(0,),
+)
 
 
 def pack_tables(table_ref, tabs):
@@ -31,7 +40,10 @@
 def look_up(tabs, e, k, idx, where_half):
     found = None
     for half in range(tabs.shape[2]):
-        piece = jnp.take_along_axis(tabs[e, k, half], idx, axis=1, mode="promise_in_bounds")
+        piece = lax.gather(
+            tabs[e, k, half], idx[:, :, None], PICK, (1, 1),
+            mode=lax.GatherScatterMode.PROMISE_IN_BOUNDS,
+        )
         found = piece if found is None else jnp.where(where_half == half, piece, found)
     return found
 
@@ -57,13 +69,15 @@
     return mix
 
 
-def tile_levels(grid_ref, tabs, weight_ref, levels, y, tile, scale):
+def tile_levels(grid_ref, tabs, weight_ref, atten_ref, levels, y, tile, scale):
     mats, planes = grid_ref.shape[:2]
+    rows = pl.ds(pl.multiple_of(tile * SUB + SUB, SUB), SUB)
     for z in range(planes):
         mid = [grid_ref[m, z, y, tile].astype(jnp.float32) for m in range(mats)]
         for e in range(weight_ref.shape[0]):
             atten = mixer(weight_ref, e)(mid)
-            level = 255.0 - 255.0 * jnp.exp(-0.5 * atten)
+            atten_ref[e, z + 1, y + 1, rows, :] = atten
+            level = 255.0 - 255.0 * jnp.exp2((-0.5 * LOG2_E) * atten)
             bin_at = level.astype(jnp.int32)
             frac = level - bin_at.astype(jnp.float32)
             w1 = frac.astype(jnp.bfloat16).astype(jnp.float32)
@@ -77,41 +91,38 @@
                 levels[y, tile, z, e * 4 + c] = value * scale if c == 3 else value
 
 
-def tile_image(dens, levels, weight_ref, y, tile, planes):
-    mats = dens.shape[0]
-    energies = weight_ref.shape[0]
+def tile_image(atten_ref, levels, y, tile, planes):
+    energies = atten_ref.shape[0]
     lane = lax.broadcasted_iota(jnp.int32, (SUB, LANES), 1)
     first, last = lane == 0, lane == LANES - 1
     base = tile * SUB + SUB
     rows = pl.ds(pl.multiple_of(base, SUB), SUB)
-    ahead = [None] * energies
-    sums = [[None] * 3 for _ in range(energies)]
-    for z in range(planes):
-        dz, dy, dx = [], [], []
-        for m in range(mats):
-            here = dens[m, z + 1, y + 1, rows, :]
-            dz.append(dens[m, z + 2, y + 1, rows, :] - dens[m, z, y + 1, rows, :])
-            dy.append(dens[m, z + 1, y + 2, rows, :] - dens[m, z + 1, y, rows, :])
-            above = dens[m, z + 1, y + 1, pl.ds(base - 1, SUB), :]
-            below = dens[m, z + 1, y + 1, pl.ds(base + 1, SUB), :]
+    sums, ahead = [], []
+    for e in range(energies):
+        clear, total = None, [None] * 3
+        for z in range(planes):
+            here = atten_ref[e, z + 1, y + 1, rows, :]
+            dz = atten_ref[e, z + 2, y + 1, rows, :] - atten_ref[e, z, y + 1, rows, :]
+            dy = atten_ref[e, z + 1, y + 2, rows, :] - atten_ref[e, z + 1, y, rows, :]
+            above = atten_ref[e, z + 1, y + 1, pl.ds(base - 1, SUB), :]
+            below = atten_ref[e, z + 1, y + 1, pl.ds(base + 1, SUB), :]
             right = pltpu.roll(jnp.where(first, below, here), LANES - 1, 1)
             left = pltpu.roll(jnp.where(last, above, here), 1, 1)
-            dx.append(right - left)
-        for e in range(energies):
-            mix = mixer(weight_ref, e)
-            gz, gy, gx = mix(dz) * 0.5, mix(dy) * 0.5, mix(dx) * 0.5
-            sq = gz * gz + gy * gy + gx * gx
-            inv = lax.rsqrt(sq + 1.0)
-            shading = 0.3 + 0.7 * jnp.abs(0.8 * gz + 0.48 * gy + 0.36 * gx) * inv
+            dx = right - left
+            sq = dz * dz + dy * dy + dx * dx
+            inv = lax.rsqrt(sq + 4.0)
+            shading = 0.3 + jnp.abs(0.56 * dz + 0.336 * dy + 0.252 * dx) * inv
             opacity = levels[y, tile, z, e * 4 + 3] * (sq * inv * inv)
             lit = opacity * shading
             if z:
-                lit = lit * ahead[e]
+                lit = lit * clear
             for c in range(3):
                 term = lit * levels[y, tile, z, e * 4 + c]
-                sums[e][c] = term if z == 0 else sums[e][c] + term
+                total[c] = term if z == 0 else total[c] + term
             transmit = 1.0 - opacity
-            ahead[e] = transmit if z == 0 else ahead[e] * transmit
+            clear = transmit if z == 0 else clear * transmit
+        sums.append(total)
+        ahead.append(clear)
     return sums, ahead
 
 
@@ -143,7 +154,7 @@
 def render_kernel(
     depth_total, mixed_hbm, table_hbm, weight_hbm, out_ref,
     mixed_ref, table_ref, weight_ref,
-    grid_ref, wide, dens, tabs, levels, z_in, y_in, image, pair_in, packed, got,
+    grid_ref, wide, atten_ref, tabs, levels, z_in, y_in, image, pair_in, packed, got,
     in_sem, up_sem, down_sem, side_sem,
     z_send, z_recv, y_send, y_recv, pair_send, pair_recv, send_sem, recv_sem,
 ):
@@ -213,29 +224,35 @@
 
     edge = jnp.zeros((SUB, LANES), jnp.float32)
     blank = jnp.zeros((strips + 2 * SUB, LANES), jnp.float32)
+
+    def clear_edges(z, carry):
+        for e in range(energies):
+            for y in range(lines):
+                atten_ref[e, z + 1, y + 1, 0:SUB, :] = edge
+                atten_ref[e, z + 1, y + 1, SUB + strips :, :] = edge
+        for side in range(2):
+            @pl.when(jnp.logical_not(has_y[side]))
+            def _():
+                for e in range(energies):
+                    atten_ref[e, z + 1, side * (lines + 1)] = blank
+        return carry
+
+    lax.fori_loop(0, planes, clear_edges, 0)
     for side in range(2):
         @pl.when(jnp.logical_not(has_z[side]))
         def _():
-            for m in range(mats):
+            for e in range(energies):
                 for y in range(lines):
-                    dens[m, side * (planes + 1), y + 1] = blank
+                    atten_ref[e, side * (planes + 1), y + 1] = blank
     loads[0].wait()
 
     def widen(z, carry):
         for m in range(mats):
             wide[m] = mixed_ref[m, z].astype(jnp.float32)
             for y in range(lines):
-                dens[m, z + 1, y + 1, 0:SUB, :] = edge
-                dens[m, z + 1, y + 1, SUB + strips :, :] = edge
                 for t in range(tiles):
                     line = wide[m, pl.ds(t * SUB * lines + y, SUB, stride=lines), :]
-                    dens[m, z + 1, y + 1, SUB + t * SUB : 2 * SUB + t * SUB, :] = line
                     grid_ref[m, z, y, t] = line.astype(grid_ref.dtype)
-        for side in range(2):
-            @pl.when(jnp.logical_not(has_y[side]))
-            def _():
-                for m in range(mats):
-                    dens[m, z + 1, side * (lines + 1)] = blank
         return carry
 
     lax.fori_loop(0, planes, widen, 0)
@@ -331,6 +348,7 @@
     pack_tables(table_ref, tabs)
     steps = tiles * lines
     every = max(1, steps // layers)
+    lag = min(LAG, steps - 1)
 
     def pass_on(p):
         for side, (turn, semaphore) in enumerate(((layers - 1 - layer, down_sem), (layer, up_sem))):
@@ -349,7 +367,7 @@
                 def _():
                     pass_on(p)
         tile_levels(
-            grid_ref, tabs, weight_ref, levels, line_of(j // tiles), j % tiles,
+            grid_ref, tabs, weight_ref, atten_ref, levels, line_of(j // tiles), j % tiles,
             6.0 / depth_total / 255.0,
         )
         return carry
@@ -365,26 +383,34 @@
         def _():
             z_copy(1 - side).wait_recv()
             for t in range(tiles):
-                for m in range(mats):
-                    for y in range(lines):
-                        dens[
-                            m, side * (planes + 1), y + 1, SUB + t * SUB : 2 * SUB + t * SUB, :
-                        ] = z_in[side, m, y, t].astype(jnp.float32)
+                for y in range(lines):
+                    mid = [z_in[side, m, y, t].astype(jnp.float32) for m in range(mats)]
+                    for e in range(energies):
+                        atten_ref[
+                            e, side * (planes + 1), y + 1, SUB + t * SUB : 2 * SUB + t * SUB, :
+                        ] = mixer(weight_ref, e)(mid)
 
     def image_step(k, carry):
+        @pl.when(k == lag)
+        def _():
+            pl.semaphore_wait(side_sem, 1)
+
+        @pl.when(k >= lag)
+        def _():
+            forward(k - lag)
+
         y, tile = line_of(k // tiles), far_first(mine, k % tiles, tiles)
         here = pl.ds(pl.multiple_of(tile * SUB + SUB, SUB), SUB)
         for side in range(2):
             @pl.when(jnp.logical_and(has_y[side], y == side * (lines - 1)))
             def _():
                 y_copy(1 - side, tile).wait_recv()
-                for m in range(mats):
-                    for z in range(planes):
-                        dens[m, z + 1, side * (lines + 1), here, :] = y_in[
-                            side, tile, m, z
-                        ].astype(jnp.float32)
-
-        sums, ahead = tile_image(dens, levels, weight_ref, y, tile, planes)
+                for z in range(planes):
+                    mid = [y_in[side, tile, m, z].astype(jnp.float32) for m in range(mats)]
+                    for e in range(energies):
+                        atten_ref[e, z + 1, side * (lines + 1), here, :] = mixer(weight_ref, e)(mid)
+
+        sums, ahead = tile_image(atten_ref, levels, y, tile, planes)
         for e in range(energies):
             for c in range(4):
                 value = sums[e][c] * (1.0 / 255.0) if c < 3 else ahead[e]
@@ -393,17 +419,15 @@
         for h in range(half_tile):
             pair_copy(y, tile * half_tile + h).start()
 
-        @pl.when(k == 1)
-        def _():
-            pl.semaphore_wait(side_sem, 1)
-
-        @pl.when(k > 0)
-        def _():
-            forward(k - 1)
         return carry
 
     lax.fori_loop(0, steps, image_step, 0)
-    forward(steps - 1)
+
+    def late_step(k, carry):
+        forward(k)
+        return carry
+
+    lax.fori_loop(steps - lag, steps, late_step, 0)
     for y in range(lines):
         got[y, pair] = packed[y, pair]
 
@@ -475,7 +499,7 @@
             pltpu.SMEM(material_weight.shape, material_weight.dtype),
             pltpu.VMEM((mats, planes, lines, tiles, SUB, LANES), density.dtype),
             pltpu.VMEM((mats, strips * lines, LANES), jnp.float32),
-            pltpu.VMEM((mats, planes + 2, lines + 2, strips + 2 * SUB, LANES), jnp.float32),
+            pltpu.VMEM((energies, planes + 2, lines + 2, strips + 2 * SUB, LANES), jnp.float32),
             pltpu.VMEM((energies, 2, color_table.shape[2] // LANES, SUB, LANES), jnp.int32),
             pltpu.VMEM((lines, tiles, planes, energies * 4, SUB, LANES), jnp.float32),
             pltpu.VMEM((2, mats, lines, tiles, SUB, LANES), density.dtype),

time: 18.9 us -> 17.2 us (0.910)
  Pallas kernels: 18.1 us -> 16.5 us
    pallas_call x1, Pallas kernels: 18.1 us -> 16.5 us  [body(): pl.pallas_call(functools.partial(render_kernel, planes * count), out_shap...]
where the time goes in v3:
time: 17.2 us; the launch traced here: 17.1 us
  Pallas kernels  16.5 us (96%)
  local copies, waits for them, and re-layouts  0.62 us (4%)
    pallas_call x1, Pallas kernels, body(): pl.pallas_call(functools.partial(render_kernel, planes * count), out_shap...  16.5 us
    unnamed x1, local copies, waits for them, and re-layouts  0.62 us

profile of v3, /device:TPU:0, one launch (start us, length us, event | category | flops | bytes accessed | tf_op | source)
XLA Modules:
  0.0 17.1 jit_solution(11739121833394968019)
XLA Ops:
  0.0 16.5 %shard_map.37 = f32[64,128]{1,0:T(8,128)S(1)} custom-call(bf16[3,8,64,128]{3,2,1,0:T(8,128)(2,1)} %bitcast.11, s32[4,4,256]{2,1,0:T(4,128)} %table_hbm.1, f32[4,3]{1,0:T(4,128)} %weight_hbm.1), custom_call_target="tpu_custom_call" | custom-call | tf_op jit(solution)/shard_map/pallas_call | solution.py:491
  16.5 0.6 %copy.7 = f32[4,4,2,256]{3,2,1,0:T(2,128)} copy(f32[4,4,2,256]{3,2,1,0:T(2,128)S(1)} %bitcast.10) | data formatting | bytes 65536

commit v4 on v3

--- a/solution.py
+++ b/solution.py
@@ -9,7 +9,7 @@
 
 LANES = 128
 SUB = 8
-LAG = 4
+LAG = 3
 LOG2_E = 1.4426950408889634
 PICK = lax.GatherDimensionNumbers(
     offset_dims=(),
@@ -155,7 +155,7 @@
     depth_total, mixed_hbm, table_hbm, weight_hbm, out_ref,
     mixed_ref, table_ref, weight_ref,
     grid_ref, wide, atten_ref, tabs, levels, z_in, y_in, image, pair_in, packed, got,
-    in_sem, up_sem, down_sem, side_sem,
+    in_sem, ready_sem,
     z_send, z_recv, y_send, y_recv, pair_send, pair_recv, send_sem, recv_sem,
 ):
     mats, planes, lines, tiles = grid_ref.shape[:4]
@@ -168,6 +168,7 @@
     stride = 4 * energies
     pieces = block // stride
     line_rows = strips * stride
+    flat = image.reshape(lines * line_rows, LANES)
     me, row = lax.axis_index("depth"), lax.axis_index("tile")
     rows_of = lax.axis_size("tile")
     has_z = (me > 0, me < count - 1)
@@ -180,8 +181,6 @@
     beside = me + 2 - 4 * (pair % 2)
     layers = pairs // 2
     layer = pair // 2
-    has_layer = (layer > 0, layer < layers - 1)
-    layer_peer = (me - 4, me + 4)
     first_line = jnp.where(has_y[0], 1, 0)
 
     def line_of(k):
@@ -217,10 +216,21 @@
         def _():
             tell(barrier, tile=y_peer[side])
 
-        @pl.when(has_layer[side])
-        def _():
-            tell(barrier, depth=layer_peer[side])
-        others = others + jnp.where(has_y[side], 1, 0) + jnp.where(has_layer[side], 1, 0)
+        others = others + jnp.where(has_y[side], 1, 0)
+
+    @pl.when(layer > 0)
+    def _():
+        tell(barrier, depth=me - 4)
+    others = others + jnp.where(layer < layers - 1, 1, 0) + 2 * layer
+
+    def tell_chips(semaphore):
+        def tell_chip(chip, carry):
+            tell(semaphore, depth=2 * chip + core)
+            return carry
+
+        return tell_chip
+
+    lax.fori_loop(2 * layer + 2, pairs, tell_chips(barrier), 0)
 
     edge = jnp.zeros((SUB, LANES), jnp.float32)
     blank = jnp.zeros((strips + 2 * SUB, LANES), jnp.float32)
@@ -278,15 +288,12 @@
             device_id_type=pl.DeviceIdType.MESH,
         )
 
-    def rows_of_block(y, owner):
-        return pl.ds(pl.multiple_of(y * line_rows + owner * block, block), block)
-
-    def pair_copy(y, chip):
+    def pair_copy(y, tile):
         return pltpu.make_async_remote_copy(
-            src_ref=image.at[rows_of_block(y, 2 * chip + 1 - core)],
-            dst_ref=pair_in.at[y, chip],
-            send_sem=pair_send.at[y, chip],
-            recv_sem=pair_recv.at[y, chip],
+            src_ref=image.at[y, pl.ds(tile * half_tile, half_tile), 1 - core],
+            dst_ref=pair_in.at[y, pl.ds(tile * half_tile, half_tile)],
+            send_sem=pair_send.at[y, tile],
+            recv_sem=pair_recv.at[y, tile],
             device_id={"depth": partner},
             device_id_type=pl.DeviceIdType.MESH,
         )
@@ -308,15 +315,14 @@
 
     def forward(k):
         y, tile = line_of(k // tiles), far_first(mine, k % tiles, tiles)
+        pair_copy(y, tile).wait_recv()
         for h in range(half_tile):
             chip = tile * half_tile + h
-            pair_copy(y, chip).wait_recv()
-            start = y * line_rows + (2 * chip + core) * block
             for s in range(pieces):
                 front, back = [], []
                 for v in range(2):
                     at = s * stride + v * SUB
-                    ours = image[pl.ds(pl.multiple_of(start + at, SUB), SUB), :]
+                    ours = image[y, chip, core, at : at + SUB, :]
                     theirs = pair_in[y, chip, at : at + SUB, :]
                     front.append(jnp.where(core == 0, ours, theirs))
                     back.append(jnp.where(core == 0, theirs, ours))
@@ -332,40 +338,24 @@
             def _():
                 block_copy(y, chip, pair).start()
 
+    lax.fori_loop(0, 2 * layer, tell_chips(ready_sem), 0)
+    for side in range(2):
+        @pl.when(has_z[side])
+        def _():
+            z_copy(side).start()
     for i in range(tiles):
         for side in range(2):
             @pl.when(has_y[side])
             def _():
                 y_copy(side, far_first(mine, i, tiles)).start()
-        if i == 0:
-            for side in range(2):
-                @pl.when(has_z[side])
-                def _():
-                    z_copy(side).start()
 
     loads[1].wait()
     loads[2].wait()
     pack_tables(table_ref, tabs)
     steps = tiles * lines
-    every = max(1, steps // layers)
-    lag = min(LAG, steps - 1)
-
-    def pass_on(p):
-        for side, (turn, semaphore) in enumerate(((layers - 1 - layer, down_sem), (layer, up_sem))):
-            @pl.when(jnp.logical_and(turn == p, has_layer[1 - side]))
-            def _():
-                pl.semaphore_wait(semaphore, 1)
-
-            @pl.when(jnp.logical_and(turn == p, has_layer[side]))
-            def _():
-                tell(semaphore, depth=layer_peer[side])
+    lag = jnp.minimum(3 + (layers - 1 - layer) // 2, steps - 1)
 
     def level_step(j, carry):
-        for p in range(layers):
-            if p * every < steps:
-                @pl.when(j == p * every)
-                def _():
-                    pass_on(p)
         tile_levels(
             grid_ref, tabs, weight_ref, atten_ref, levels, line_of(j // tiles), j % tiles,
             6.0 / depth_total / 255.0,
@@ -373,10 +363,6 @@
         return carry
 
     lax.fori_loop(0, steps, level_step, 0)
-    for p in range(layers):
-        if p * every >= steps:
-            pass_on(p)
-    tell(side_sem, depth=beside)
 
     for side in range(2):
         @pl.when(has_z[side])
@@ -391,9 +377,9 @@
                         ] = mixer(weight_ref, e)(mid)
 
     def image_step(k, carry):
-        @pl.when(k == lag)
-        def _():
-            pl.semaphore_wait(side_sem, 1)
+        @pl.when(jnp.logical_and(k == lag, layer < layers - 1))
+        def _():
+            pl.semaphore_wait(ready_sem, 2 * (layers - 1 - layer))
 
         @pl.when(k >= lag)
         def _():
@@ -415,9 +401,8 @@
             for c in range(4):
                 value = sums[e][c] * (1.0 / 255.0) if c < 3 else ahead[e]
                 start = y * line_rows + tile * (SUB * stride) + c * energies + e
-                image[pl.ds(start, SUB, stride=stride), :] = value
-        for h in range(half_tile):
-            pair_copy(y, tile * half_tile + h).start()
+                flat[pl.ds(start, SUB, stride=stride), :] = value
+        pair_copy(y, tile).start()
 
         return carry
 
@@ -464,9 +449,9 @@
             for t in range(tiles):
                 y_copy(side, t).wait_send()
     for y in range(lines):
+        for t in range(tiles):
+            pair_copy(y, t).wait_send()
         for n in range(pairs):
-            pair_copy(y, n).wait_send()
-
             @pl.when(pair != n)
             def _():
                 block_copy(y, n, n).wait_send()
@@ -504,13 +489,13 @@
             pltpu.VMEM((lines, tiles, planes, energies * 4, SUB, LANES), jnp.float32),
             pltpu.VMEM((2, mats, lines, tiles, SUB, LANES), density.dtype),
             pltpu.VMEM((2, tiles, mats, planes, SUB, LANES), density.dtype),
-            pltpu.VMEM((total, LANES), jnp.float32),
+            pltpu.VMEM((lines, pairs, 2, block, LANES), jnp.float32),
             pltpu.VMEM((lines, pairs, block, LANES), jnp.float32),
             pltpu.VMEM((lines, pairs, block, LANES), wire),
             pltpu.VMEM((lines, pairs, block, LANES), wire),
-            dma((3,)), flag, flag, flag,
+            dma((3,)), flag,
             dma((2,)), dma((2,)), dma((2, tiles)), dma((2, tiles)),
-            dma((lines, pairs)), dma((lines, pairs)), dma((lines, pairs)), dma((lines, pairs)),
+            dma((lines, tiles)), dma((lines, tiles)), dma((lines, pairs)), dma((lines, pairs)),
         ],
         compiler_params=pltpu.CompilerParams(collective_id=0, has_side_effects=True),
     )(mixed, color_table, material_weight)

time: 17.2 us -> 16.7 us (0.971)
  Pallas kernels: 16.5 us -> 16 us
    pallas_call x1, Pallas kernels: 16.5 us -> 16 us  [body(): pl.pallas_call(functools.partial(render_kernel, planes * count), out_shap...]
where the time goes in v4:
time: 16.7 us; the launch traced here: 16.6 us
  Pallas kernels  16 us (96%)
  local copies, waits for them, and re-layouts  0.62 us (4%)
    pallas_call x1, Pallas kernels, body(): pl.pallas_call(functools.partial(render_kernel, planes * count), out_shap...  16 us
    unnamed x1, local copies, waits for them, and re-layouts  0.62 us

profile of v4, /device:TPU:0, one launch (start us, length us, event | category | flops | bytes accessed | tf_op | source)
XLA Modules:
  0.0 16.6 jit_solution(3908898078911572369)
XLA Ops:
  0.0 16.0 %shard_map.37 = f32[64,128]{1,0:T(8,128)S(1)} custom-call(bf16[3,8,64,128]{3,2,1,0:T(8,128)(2,1)} %bitcast.11, s32[4,4,256]{2,1,0:T(4,128)} %table_hbm.1, f32[4,3]{1,0:T(4,128)} %weight_hbm.1), custom_call_target="tpu_custom_call" | custom-call | tf_op jit(solution)/shard_map/pallas_call | solution.py:476
  16.0 0.6 %copy.7 = f32[4,4,2,256]{3,2,1,0:T(2,128)} copy(f32[4,4,2,256]{3,2,1,0:T(2,128)S(1)} %bitcast.10) | data formatting | bytes 65536
